TPU v7x, 32 devices: a whole 2x2x4 slice. The times are simulated.
32 devices in a mesh: sky: 2 (over x), vel: 16 (over z, y, core).
Axes of the slice: x: 2, y: 2, z: 4, core: 2. Of those that a mesh axis runs over, the one named last changes fastest.
Arguments:
- psi: bfloat16 [2, 512, 1024], P(None, 'vel', 'sky'), may hold values from -6 to 6
- phi: bfloat16 [2, 512, 1024], P(None, 'vel', 'sky'), may hold values from 0.25 to 4
- shifts: int32 [512, 2, 2], P('vel'), may hold values from -16 to 16, as said below
- tile_mask: int32 [2, 2], replicated, may hold values 0 or 1
Outputs:
- best: float32 [512, 1024], P('vel', 'sky')
Inputs may be any that keep to these rules, and one draw needn't show every extreme that they name: `shifts`: pixel offsets of an epoch's image; entry 0 is a row offset, entry 1 a column offset.
All inputs are finite; a program needn't handle non-finite values.
Results may differ from a plain program's by a relative error of at most 0.0003.
Values may be sent and summed in bfloat16 or wider, within the bound.
No kernel may reach another device: no remote copies, remote signals or barrier semaphores. Data moves between devices by JAX's collectives and lax.ppermute only.
A program may use at most 64 MiB of HBM per device.

v0:
```python
import jax
import jax.numpy as jnp
from jax import lax
from jax.sharding import PartitionSpec as P

MAXS = 16


def padded_2(block, sides, width):
    for axis, dim in sides:
        count = lax.axis_size(axis)
        forward = [(i, i + 1) for i in range(count - 1)]
        backward = [(target, source) for source, target in forward]
        low = lax.ppermute(
            lax.slice_in_dim(block, block.shape[dim] - width, None, axis=dim), axis, forward
        )
        high = lax.ppermute(lax.slice_in_dim(block, 0, width, axis=dim), axis, backward)
        block = jnp.concatenate([low, block, high], axis=dim)
    return block


def stack_best(padded, offset_table, height, breadth, margin):
    total_vel = offset_table.shape[0]
    epochs = padded.shape[1]
    per_step = 1
    while total_vel // per_step > 16 or total_vel % per_step:
        per_step += 1
    grouped = offset_table.reshape(total_vel // per_step, per_step, epochs, 2)

    def advance(record, offsets):
        for member in range(per_step):
            psi_total = jnp.zeros((height, breadth), jnp.float32)
            phi_total = jnp.zeros((height, breadth), jnp.float32)
            for epoch in range(epochs):
                row_at = margin + offsets[member, epoch, 0]
                col_at = margin + offsets[member, epoch, 1]
                psi_total = psi_total + lax.dynamic_slice(
                    padded[0, epoch], (row_at, col_at), (height, breadth)
                ).astype(jnp.float32)
                phi_total = phi_total + lax.dynamic_slice(
                    padded[1, epoch], (row_at, col_at), (height, breadth)
                ).astype(jnp.float32)
            record = jnp.maximum(record, psi_total / jnp.sqrt(jnp.maximum(phi_total, 1.0)))
        return (record, None)

    start = jnp.full((height, breadth), -1e30, jnp.float32)
    record, unused = lax.scan(advance, start, grouped)
    return record


def body(psi, phi, shifts, tile_mask):
    margin = MAXS
    height = psi.shape[1]
    breadth = psi.shape[2]
    sky_index = lax.axis_index("sky")
    keep = lax.dynamic_slice_in_dim(tile_mask, sky_index, 1, 1).astype(jnp.bfloat16)[:, :, None]
    stacked = jnp.stack([psi * keep, phi * keep])
    whole = lax.all_gather(stacked, "vel", axis=2, tiled=True)
    rimmed = padded_2(whole, (("sky", 3),), margin)
    padded = jnp.pad(rimmed, ((0, 0), (0, 0), (margin, margin), (0, 0)))
    full_height = rimmed.shape[2]
    record = stack_best(padded, shifts, full_height, breadth, margin)
    joined = lax.pmax(record, "vel")
    result = lax.dynamic_slice_in_dim(joined, lax.axis_index("vel") * height, height, 0)
    return result


def solution(mesh):
    placed = (P(None, "vel", "sky"), P(None, "vel", "sky"), P("vel", None, None), P())
    return jax.shard_map(
        body, mesh=mesh, in_specs=placed, out_specs=P("vel", "sky"), check_vma=False
    )
```

profile of v0, /device:TPU:0, one launch (start us, length us, event | category | flops | bytes accessed | tf_op | source)
XLA Modules:
  0.0 437.1 jit_solution(14862448438077397219)
XLA Ops:
  9.1 44.6 %all-gather.2.cloned.1.call-done = bf16[2,2,512,512]{3,2,1,0:T(8,128)(2,1)} async-done(((bf16[2,2,32,512]{3,2,1,0:T(8,128)(2,1)}), bf16[2,2,512,512]{3,2,1,0:T(8,128)(2,1)}) %all-gather.2.cloned.1.call-update) | async-done | bytes 2097168 | tf_op jit(solution)/shard_map/all_gather | solution.py:58
  55.1 3.4 collective-permute-start
  60.0 10.1 %collective-permute-done = bf16[2,2,512,16]{3,2,1,0:T(8,128)(2,1)S(1)} collective-permute-done((bf16[2,2,512,16]{3,2,1,0:T(8,128)(2,1)S(1)}, bf16[2,2,512,16]{3,2,1,0:T(8,128)(2,1)S(1)}, u32[]{:S(2)}, u32[]{:S(2)}) %collective-permute-start) | collective-permute-done | bytes 65568 | tf_op jit(solution)/shard_map/ppermute | solution.py:14
  70.1 4.3 collective-permute-done.1
  74.4 3.1 fusion.6
  77.5 259.4 %while.14 = (s32[]{:T(128)}, f32[512,512]{1,0:T(8,128)}, bf16[2,2,544,544]{3,2,1,0:T(8,128)(2,1)S(1)}, s32[16,2,2,2]{3,2,1,0:T(2,128)S(1)}, s32[]{:T(128)}, /*in...) while((s32[]{:T(128)}, f32[512,512]{1,0:T(8,128)}, bf16[2,2,544,544]{3,2,1,0:T(8,128)(2,1)S(1)}, ...), condition=%wide.region_1.2_spmd.clone, body=%wide.region_0.1_spmd.clone.sunk | while | flops 4980771 | bytes 19415732 | solution.py:47
  89.2 3.5 bitcast_maximum_fusion.3
  105.4 3.5 bitcast_maximum_fusion.3
  121.6 3.5 bitcast_maximum_fusion.3
  137.8 3.5 bitcast_maximum_fusion.3
  154.0 3.5 bitcast_maximum_fusion.3
  170.2 3.5 bitcast_maximum_fusion.3
  186.4 3.5 bitcast_maximum_fusion.3
  202.6 3.5 bitcast_maximum_fusion.3
  218.8 3.5 bitcast_maximum_fusion.3
  235.0 3.6 bitcast_maximum_fusion.3
  251.3 3.6 bitcast_maximum_fusion.3
  267.5 3.5 bitcast_maximum_fusion.3
  283.7 3.5 bitcast_maximum_fusion.3
  299.9 3.5 bitcast_maximum_fusion.3
  316.1 3.5 bitcast_maximum_fusion.3
  332.3 3.5 bitcast_maximum_fusion.3
  336.9 91.9 %all-reduce.3.cloned.1.call-done = f32[512,512]{1,0:T(8,128)} async-done(((f32[512,512]{1,0:T(8,128)}), f32[512,512]{1,0:T(8,128)}) %all-reduce.3.cloned.1.call-update) | async-done | bytes 1048592 | tf_op jit(solution)/shard_map/pmax | solution.py:63
  428.8 1.5 constant_dynamic-slice_fusion.1
  (125 shorter events, 51.0 us)
Async XLA Ops:
  6.5 53.3 %copy-start.2 = (s32[32,2,2]{0,2,1:T(2,128)S(1)}, s32[32,2,2]{0,2,1:T(2,128)}, u32[]{:S(2)}) copy-start(s32[32,2,2]{0,2,1:T(2,128)} %param.8) | copy-start | bytes 1540
  6.5 47.2 %all-gather.2.cloned.1.call-start = ((), (), s32[]{:S(2)}) async-start(), calls=%async_computation | async-start | bytes 2228224 | tf_op jit(solution)/shard_map/all_gather | solution.py:58
  9.1 419.7 %all-reduce.3.cloned.1.call-start = ((), (), s32[]{:S(2)}) async-start(), calls=%async_computation.1 | async-start | bytes 2097152 | tf_op jit(solution)/shard_map/pmax | solution.py:63
  55.1 15.0 %collective-permute-start = (bf16[2,2,512,16]{3,2,1,0:T(8,128)(2,1)S(1)}, bf16[2,2,512,16]{3,2,1,0:T(8,128)(2,1)S(1)}, u32[]{:S(2)}, u32[]{:S(2)}) collective-permute-start(bf16[2,2,512,16]{3,2,1,0:T(8,128)(2,1)S(1)} %get-tuple-element.122), channel_id=1, source_target_pairs={{0,16},{1,17},{2,18},{3,19},{4,20},{5,21},{6,22},{7,23},{8,24},{9,... | collective-permute-start | bytes 196616 | tf_op jit(solution)/shard_map/ppermute | solution.py:14
  58.5 15.8 %collective-permute-start.1 = (bf16[2,2,512,16]{3,2,1,0:T(8,128)(2,1)S(1)}, bf16[2,2,512,16]{3,2,1,0:T(8,128)(2,1)}, u32[]{:S(2)}, u32[]{:S(2)}) collective-permute-start(bf16[2,2,512,16]{3,2,1,0:T(8,128)(2,1)S(1)} %get-tuple-element.123), channel_id=1, source_target_pairs={{16,0},{17,1},{18,2},{19,3},{20,4},{21,5},{22,6},{23,7},{24,8},{25... | collective-permute-start | bytes 196616 | tf_op jit(solution)/shard_map/ppermute | solution.py:17
  88.0 1.2 copy-start
  104.2 1.2 copy-start
  120.4 1.2 copy-start
  125.1 1.0 copy-start.1
  136.6 1.2 copy-start
  152.8 1.2 copy-start
  169.0 1.2 copy-start
  185.2 1.2 copy-start
  201.4 1.2 copy-start
  217.6 1.2 copy-start
  222.4 1.0 copy-start.1
  233.8 1.2 copy-start
  238.6 1.0 copy-start.1
  250.0 1.2 copy-start
  266.2 1.2 copy-start
  282.5 1.2 copy-start
  298.7 1.2 copy-start
  314.9 1.2 copy-start
  331.1 1.2 copy-start
  (13 other events, 12.9 us)
Sparse Core Ops, SparseCore 0:
  9.5 44.1 all-gather.1
  337.0 91.7 all-reduce.2
where the time goes:
time: 440 us; the launch traced here: 437 us
  loops' own time  157 us (36%)
  waiting for transfers between devices  151 us (34%)
  other arithmetic  62.2 us (14%)
  local copies, waits for them, and re-layouts  48.6 us (11%)
  between operations  13.5 us (3%)
  starting transfers between devices  4.74 us (1%)
    another operation x1, loops' own time, stack_best(): record, unused = lax.scan(advance, start, grouped)  157 us
    pmax x1, waiting for transfers between devices, body(): joined = lax.pmax(record, 'vel')  91.9 us
    max x16, other arithmetic, advance(): jnp.maximum(record, psi_total / jnp.sqrt(jnp.maximum(phi_total, 1.0)))  56.6 us
    all_gather x1, waiting for transfers between devices, body(): whole = lax.all_gather(stacked, 'vel', axis=2, tiled=True)  44.6 us
    while x64, local copies, waits for them, and re-layouts  31.2 us
    slice x16, local copies, waits for them, and re-layouts, advance(): col_at = margin + offsets[member, epoch, 1]  10.5 us
    ppermute x1, waiting for transfers between devices, padded_2(): lax.ppermute(lax.slice_in_dim(block, block.shape[dim] - width, None, axis...  10.1 us
  transfers between devices with their start and end apart: 4, of which 4 were waited for; matrix products, arithmetic and copies ran while one was open for 0% of the time, Pallas kernels for 0%

commit v1 on v0

--- a/solution.py
+++ b/solution.py
@@ -4,6 +4,19 @@
 from jax.sharding import PartitionSpec as P
 
 MAXS = 16
+
+
+def post_the_results(buf):
+    q_n = lax.axis_size("vel")
+    samples = list(map(lambda at: (at, (at + 1) % q_n), range(q_n)))
+
+    def lines_hold(u1):
+        if len(u1) == q_n:
+            return u1
+        return lines_hold([lax.ppermute(u1[0], "vel", samples), *u1])
+
+    near = jnp.concatenate(lines_hold([buf]), axis=2)
+    return jnp.roll(near, shift=(lax.axis_index("vel") + 1) * buf.shape[2], axis=2)
 
 
 def padded_2(block, sides, width):
@@ -55,7 +68,7 @@
     sky_index = lax.axis_index("sky")
     keep = lax.dynamic_slice_in_dim(tile_mask, sky_index, 1, 1).astype(jnp.bfloat16)[:, :, None]
     stacked = jnp.stack([psi * keep, phi * keep])
-    whole = lax.all_gather(stacked, "vel", axis=2, tiled=True)
+    whole = post_the_results(stacked)
     rimmed = padded_2(whole, (("sky", 3),), margin)
     padded = jnp.pad(rimmed, ((0, 0), (0, 0), (margin, margin), (0, 0)))
     full_height = rimmed.shape[2]

time: 440 us -> 528 us (1.20)
  waiting for transfers between devices: 151 us -> 206 us
  other arithmetic: 62.2 us -> 95.6 us
    ppermute x0 -> x15, waiting for transfers between devices: none -> 106 us  [lines_hold(): return lines_hold([lax.ppermute(u1[0], 'vel', samples), *u1])]
    all_gather x1 -> x0, waiting for transfers between devices: 44.6 us -> none  [body(): whole = lax.all_gather(stacked, 'vel', axis=2, tiled=True)]
    max x16, other arithmetic: 56.6 us -> 90.8 us  [advance(): jnp.maximum(record, psi_total / jnp.sqrt(jnp.maximum(phi_total, 1.0)))]
    while x64 -> x0, local copies, waits for them, and re-layouts: 31.2 us -> none
    slice x16, local copies, waits for them, and re-layouts: 3.87 us -> 31.6 us  [advance(): padded[0, epoch]]
  transfers between devices with their start and end apart: 4 -> 18, of which waited for: 4 -> 18; matrix products, arithmetic and copies ran while one was open for 0% -> 0% of each run, Pallas kernels for 0% -> 0%
where the time goes in v1:
time: 528 us; the launch traced here: 524 us
  waiting for transfers between devices  206 us (39%)
  loops' own time  158 us (30%)
  other arithmetic  95.6 us (18%)
  local copies, waits for them, and re-layouts  45.5 us (9%)
  between operations  13.7 us (3%)
  starting transfers between devices  5.7 us (1%)
    another operation x1, loops' own time, stack_best(): record, unused = lax.scan(advance, start, grouped)  158 us
    ppermute x15, waiting for transfers between devices, lines_hold(): return lines_hold([lax.ppermute(u1[0], 'vel', samples), *u1])  106 us
    max x16, other arithmetic, advance(): jnp.maximum(record, psi_total / jnp.sqrt(jnp.maximum(phi_total, 1.0)))  90.8 us
    pmax x1, waiting for transfers between devices, body(): joined = lax.pmax(record, 'vel')  90.1 us
    slice x16, local copies, waits for them, and re-layouts, advance(): padded[0, epoch]  31.6 us
    slice x16, local copies, waits for them, and re-layouts, advance(): col_at = margin + offsets[member, epoch, 1]  10.9 us
  transfers between devices with their start and end apart: 18, of which 18 were waited for; matrix products, arithmetic and copies ran while one was open for 0% of the time, Pallas kernels for 0%

profile of v1, /device:TPU:0, one launch (start us, length us, event | category | flops | bytes accessed | tf_op | source)
XLA Modules:
  0.0 524.2 jit_solution(6732705180513405737)
XLA Ops:
  8.9 7.6 %collective-permute-done = bf16[2,2,32,512]{3,2,1,0:T(8,128)(2,1)S(1)} collective-permute-done((bf16[2,2,32,512]{3,2,1,0:T(8,128)(2,1)S(1)}, bf16[2,2,32,512]{3,2,1,0:T(8,128)(2,1)S(1)}, u32[]{:S(2)}, u32[]{:S(2)}) %collective-permute-start) | collective-permute-done | bytes 131104 | tf_op jit(solution)/shard_map/ppermute | solution.py:16
  16.5 7.1 %collective-permute-done.1 = bf16[2,2,32,512]{3,2,1,0:T(8,128)(2,1)S(1)} collective-permute-done((bf16[2,2,32,512]{3,2,1,0:T(8,128)(2,1)S(1)}, bf16[2,2,32,512]{3,2,1,0:T(8,128)(2,1)S(1)}, u32[]{:S(2)}, u32[]{:S(2)}) %collective-permute-start.1) | collective-permute-done | bytes 131104 | tf_op jit(solution)/shard_map/ppermute | solution.py:16
  23.6 7.1 %collective-permute-done.2 = bf16[2,2,32,512]{3,2,1,0:T(8,128)(2,1)S(1)} collective-permute-done((bf16[2,2,32,512]{3,2,1,0:T(8,128)(2,1)S(1)}, bf16[2,2,32,512]{3,2,1,0:T(8,128)(2,1)S(1)}, u32[]{:S(2)}, u32[]{:S(2)}) %collective-permute-start.2) | collective-permute-done | bytes 131104 | tf_op jit(solution)/shard_map/ppermute | solution.py:16
  30.7 7.1 %collective-permute-done.3 = bf16[2,2,32,512]{3,2,1,0:T(8,128)(2,1)S(1)} collective-permute-done((bf16[2,2,32,512]{3,2,1,0:T(8,128)(2,1)S(1)}, bf16[2,2,32,512]{3,2,1,0:T(8,128)(2,1)S(1)}, u32[]{:S(2)}, u32[]{:S(2)}) %collective-permute-start.3) | collective-permute-done | bytes 131104 | tf_op jit(solution)/shard_map/ppermute | solution.py:16
  37.8 7.1 %collective-permute-done.4 = bf16[2,2,32,512]{3,2,1,0:T(8,128)(2,1)S(1)} collective-permute-done((bf16[2,2,32,512]{3,2,1,0:T(8,128)(2,1)S(1)}, bf16[2,2,32,512]{3,2,1,0:T(8,128)(2,1)S(1)}, u32[]{:S(2)}, u32[]{:S(2)}) %collective-permute-start.4) | collective-permute-done | bytes 131104 | tf_op jit(solution)/shard_map/ppermute | solution.py:16
  44.9 7.1 %collective-permute-done.5 = bf16[2,2,32,512]{3,2,1,0:T(8,128)(2,1)S(1)} collective-permute-done((bf16[2,2,32,512]{3,2,1,0:T(8,128)(2,1)S(1)}, bf16[2,2,32,512]{3,2,1,0:T(8,128)(2,1)S(1)}, u32[]{:S(2)}, u32[]{:S(2)}) %collective-permute-start.5) | collective-permute-done | bytes 131104 | tf_op jit(solution)/shard_map/ppermute | solution.py:16
  52.0 7.1 %collective-permute-done.6 = bf16[2,2,32,512]{3,2,1,0:T(8,128)(2,1)S(1)} collective-permute-done((bf16[2,2,32,512]{3,2,1,0:T(8,128)(2,1)S(1)}, bf16[2,2,32,512]{3,2,1,0:T(8,128)(2,1)S(1)}, u32[]{:S(2)}, u32[]{:S(2)}) %collective-permute-start.6) | collective-permute-done | bytes 131104 | tf_op jit(solution)/shard_map/ppermute | solution.py:16
  59.1 7.1 %collective-permute-done.7 = bf16[2,2,32,512]{3,2,1,0:T(8,128)(2,1)S(1)} collective-permute-done((bf16[2,2,32,512]{3,2,1,0:T(8,128)(2,1)S(1)}, bf16[2,2,32,512]{3,2,1,0:T(8,128)(2,1)S(1)}, u32[]{:S(2)}, u32[]{:S(2)}) %collective-permute-start.7) | collective-permute-done | bytes 131104 | tf_op jit(solution)/shard_map/ppermute | solution.py:16
  66.2 7.1 %collective-permute-done.8 = bf16[2,2,32,512]{3,2,1,0:T(8,128)(2,1)S(1)} collective-permute-done((bf16[2,2,32,512]{3,2,1,0:T(8,128)(2,1)S(1)}, bf16[2,2,32,512]{3,2,1,0:T(8,128)(2,1)S(1)}, u32[]{:S(2)}, u32[]{:S(2)}) %collective-permute-start.8) | collective-permute-done | bytes 131104 | tf_op jit(solution)/shard_map/ppermute | solution.py:16
  73.3 7.1 %collective-permute-done.9 = bf16[2,2,32,512]{3,2,1,0:T(8,128)(2,1)S(1)} collective-permute-done((bf16[2,2,32,512]{3,2,1,0:T(8,128)(2,1)S(1)}, bf16[2,2,32,512]{3,2,1,0:T(8,128)(2,1)S(1)}, u32[]{:S(2)}, u32[]{:S(2)}) %collective-permute-start.9) | collective-permute-done | bytes 131104 | tf_op jit(solution)/shard_map/ppermute | solution.py:16
  80.3 7.1 %collective-permute-done.10 = bf16[2,2,32,512]{3,2,1,0:T(8,128)(2,1)S(1)} collective-permute-done((bf16[2,2,32,512]{3,2,1,0:T(8,128)(2,1)S(1)}, bf16[2,2,32,512]{3,2,1,0:T(8,128)(2,1)S(1)}, u32[]{:S(2)}, u32[]{:S(2)}) %collective-permute-start.10) | collective-permute-done | bytes 131104 | tf_op jit(solution)/shard_map/ppermute | solution.py:16
  87.4 7.1 %collective-permute-done.11 = bf16[2,2,32,512]{3,2,1,0:T(8,128)(2,1)S(1)} collective-permute-done((bf16[2,2,32,512]{3,2,1,0:T(8,128)(2,1)S(1)}, bf16[2,2,32,512]{3,2,1,0:T(8,128)(2,1)S(1)}, u32[]{:S(2)}, u32[]{:S(2)}) %collective-permute-start.11) | collective-permute-done | bytes 131104 | tf_op jit(solution)/shard_map/ppermute | solution.py:16
  94.5 7.1 %collective-permute-done.12 = bf16[2,2,32,512]{3,2,1,0:T(8,128)(2,1)S(1)} collective-permute-done((bf16[2,2,32,512]{3,2,1,0:T(8,128)(2,1)S(1)}, bf16[2,2,32,512]{3,2,1,0:T(8,128)(2,1)S(1)}, u32[]{:S(2)}, u32[]{:S(2)}) %collective-permute-start.12) | collective-permute-done | bytes 131104 | tf_op jit(solution)/shard_map/ppermute | solution.py:16
  101.6 7.1 %collective-permute-done.13 = bf16[2,2,32,512]{3,2,1,0:T(8,128)(2,1)S(1)} collective-permute-done((bf16[2,2,32,512]{3,2,1,0:T(8,128)(2,1)S(1)}, bf16[2,2,32,512]{3,2,1,0:T(8,128)(2,1)S(1)}, u32[]{:S(2)}, u32[]{:S(2)}) %collective-permute-start.13) | collective-permute-done | bytes 131104 | tf_op jit(solution)/shard_map/ppermute | solution.py:16
  109.5 6.3 %collective-permute-done.14 = bf16[2,2,32,512]{3,2,1,0:T(8,128)(2,1)S(1)} collective-permute-done((bf16[2,2,32,512]{3,2,1,0:T(8,128)(2,1)S(1)}, bf16[2,2,32,512]{3,2,1,0:T(8,128)(2,1)S(1)}, u32[]{:S(2)}, u32[]{:S(2)}) %collective-permute-start.14) | collective-permute-done | bytes 131104 | tf_op jit(solution)/shard_map/ppermute | solution.py:16
  134.6 291.2 %while.14 = (s32[]{:T(128)}, f32[512,512]{1,0:T(8,128)}, bf16[2,2,544,544]{3,2,1,0:T(8,128)(2,1)}, s32[16,2,2,2]{3,2,1,0:T(2,128)S(1)}, s32[]{:T(128)}, /*index=...) while((s32[]{:T(128)}, f32[512,512]{1,0:T(8,128)}, bf16[2,2,544,544]{3,2,1,0:T(8,128)(2,1)}, ...), condition=%wide.region_1.2_spmd.clone, body=%wide.region_0.1_spmd.clone.sunk | while | flops 4980771 | bytes 11027059 | solution.py:60
  164.1 5.8 %bitcast_maximum_fusion.3 = f32[512,512]{1,0:T(8,128)} fusion(f32[512,512]{1,0:T(8,128)} %get-tuple-element.184, bf16[1,1,544,544]{3,2,1,0:T(8,128)(2,1)S(1)} %get-tuple-element.163, s32[]{:T(128)S(6)} %select_n.103, s32[]{:T(128)S(6)} %select_n.104, bf16[1,1,544,544]{3,2,1,0:T(8,128)(2,1)S(1)} %get-tuple-element.166, s32[]{:T(128)S(6)} %select_n.105, ...), kind=kLoop, calls=%fused_computation.clone.1 | loop fusion | flops 4980736 | bytes 6291489 | tf_op jit(solution)/shard_map/while/body/eval_jaxpr/max | solution.py:56
  200.7 5.8 %bitcast_maximum_fusion.3 = f32[512,512]{1,0:T(8,128)} fusion(f32[512,512]{1,0:T(8,128)} %get-tuple-element.184, bf16[1,1,544,544]{3,2,1,0:T(8,128)(2,1)S(1)} %get-tuple-element.163, s32[]{:T(128)S(6)} %select_n.103, s32[]{:T(128)S(6)} %select_n.104, bf16[1,1,544,544]{3,2,1,0:T(8,128)(2,1)S(1)} %get-tuple-element.166, s32[]{:T(128)S(6)} %select_n.105, ...), kind=kLoop, calls=%fused_computation.clone.1 | loop fusion | flops 4980736 | bytes 6291489 | tf_op jit(solution)/shard_map/while/body/eval_jaxpr/max | solution.py:56
  219.0 5.8 %bitcast_maximum_fusion.3 = f32[512,512]{1,0:T(8,128)} fusion(f32[512,512]{1,0:T(8,128)} %get-tuple-element.184, bf16[1,1,544,544]{3,2,1,0:T(8,128)(2,1)S(1)} %get-tuple-element.163, s32[]{:T(128)S(6)} %select_n.103, s32[]{:T(128)S(6)} %select_n.104, bf16[1,1,544,544]{3,2,1,0:T(8,128)(2,1)S(1)} %get-tuple-element.166, s32[]{:T(128)S(6)} %select_n.105, ...), kind=kLoop, calls=%fused_computation.clone.1 | loop fusion | flops 4980736 | bytes 6291489 | tf_op jit(solution)/shard_map/while/body/eval_jaxpr/max | solution.py:56
  237.3 5.8 %bitcast_maximum_fusion.3 = f32[512,512]{1,0:T(8,128)} fusion(f32[512,512]{1,0:T(8,128)} %get-tuple-element.184, bf16[1,1,544,544]{3,2,1,0:T(8,128)(2,1)S(1)} %get-tuple-element.163, s32[]{:T(128)S(6)} %select_n.103, s32[]{:T(128)S(6)} %select_n.104, bf16[1,1,544,544]{3,2,1,0:T(8,128)(2,1)S(1)} %get-tuple-element.166, s32[]{:T(128)S(6)} %select_n.105, ...), kind=kLoop, calls=%fused_computation.clone.1 | loop fusion | flops 4980736 | bytes 6291489 | tf_op jit(solution)/shard_map/while/body/eval_jaxpr/max | solution.py:56
  255.5 5.8 %bitcast_maximum_fusion.3 = f32[512,512]{1,0:T(8,128)} fusion(f32[512,512]{1,0:T(8,128)} %get-tuple-element.184, bf16[1,1,544,544]{3,2,1,0:T(8,128)(2,1)S(1)} %get-tuple-element.163, s32[]{:T(128)S(6)} %select_n.103, s32[]{:T(128)S(6)} %select_n.104, bf16[1,1,544,544]{3,2,1,0:T(8,128)(2,1)S(1)} %get-tuple-element.166, s32[]{:T(128)S(6)} %select_n.105, ...), kind=kLoop, calls=%fused_computation.clone.1 | loop fusion | flops 4980736 | bytes 6291489 | tf_op jit(solution)/shard_map/while/body/eval_jaxpr/max | solution.py:56
  292.1 5.8 %bitcast_maximum_fusion.3 = f32[512,512]{1,0:T(8,128)} fusion(f32[512,512]{1,0:T(8,128)} %get-tuple-element.184, bf16[1,1,544,544]{3,2,1,0:T(8,128)(2,1)S(1)} %get-tuple-element.163, s32[]{:T(128)S(6)} %select_n.103, s32[]{:T(128)S(6)} %select_n.104, bf16[1,1,544,544]{3,2,1,0:T(8,128)(2,1)S(1)} %get-tuple-element.166, s32[]{:T(128)S(6)} %select_n.105, ...), kind=kLoop, calls=%fused_computation.clone.1 | loop fusion | flops 4980736 | bytes 6291489 | tf_op jit(solution)/shard_map/while/body/eval_jaxpr/max | solution.py:56
  383.4 5.8 %bitcast_maximum_fusion.3 = f32[512,512]{1,0:T(8,128)} fusion(f32[512,512]{1,0:T(8,128)} %get-tuple-element.184, bf16[1,1,544,544]{3,2,1,0:T(8,128)(2,1)S(1)} %get-tuple-element.163, s32[]{:T(128)S(6)} %select_n.103, s32[]{:T(128)S(6)} %select_n.104, bf16[1,1,544,544]{3,2,1,0:T(8,128)(2,1)S(1)} %get-tuple-element.166, s32[]{:T(128)S(6)} %select_n.105, ...), kind=kLoop, calls=%fused_computation.clone.1 | loop fusion | flops 4980736 | bytes 6291489 | tf_op jit(solution)/shard_map/while/body/eval_jaxpr/max | solution.py:56
  425.8 90.1 %all-reduce.3.cloned.1.call-done = f32[512,512]{1,0:T(8,128)} async-done(((f32[512,512]{1,0:T(8,128)}), f32[512,512]{1,0:T(8,128)}) %all-reduce.3.cloned.1.call-update) | async-done | bytes 1048592 | tf_op jit(solution)/shard_map/pmax | solution.py:76
  (119 shorter events, 116.1 us)
Async XLA Ops:
  6.5 509.3 %all-reduce.3.cloned.1.call-start = ((), (), s32[]{:S(2)}) async-start(), calls=%async_computation | async-start | bytes 2097152 | tf_op jit(solution)/shard_map/pmax | solution.py:76
  8.4 8.2 %collective-permute-start = (bf16[2,2,32,512]{3,2,1,0:T(8,128)(2,1)S(1)}, bf16[2,2,32,512]{3,2,1,0:T(8,128)(2,1)S(1)}, u32[]{:S(2)}, u32[]{:S(2)}) collective-permute-start(bf16[2,2,32,512]{3,2,1,0:T(8,128)(2,1)S(1)} %pad_maximum_fusion), channel_id=1, source_target_pairs={{0,1},{1,2},{2,3},{3,4},{4,5},{5,6},{6,7},{7,8},{8,9},{9,10},{10,1... | collective-permute-start | bytes 393224 | tf_op jit(solution)/shard_map/ppermute | solution.py:16
  16.5 7.1 %collective-permute-start.1 = (bf16[2,2,32,512]{3,2,1,0:T(8,128)(2,1)S(1)}, bf16[2,2,32,512]{3,2,1,0:T(8,128)(2,1)S(1)}, u32[]{:S(2)}, u32[]{:S(2)}) collective-permute-start(bf16[2,2,32,512]{3,2,1,0:T(8,128)(2,1)S(1)} %collective-permute-done), channel_id=1, source_target_pairs={{0,1},{1,2},{2,3},{3,4},{4,5},{5,6},{6,7},{7,8},{8,9},{9,10},{10,1... | collective-permute-start | bytes 393224 | tf_op jit(solution)/shard_map/ppermute | solution.py:16
  23.6 7.1 %collective-permute-start.2 = (bf16[2,2,32,512]{3,2,1,0:T(8,128)(2,1)S(1)}, bf16[2,2,32,512]{3,2,1,0:T(8,128)(2,1)S(1)}, u32[]{:S(2)}, u32[]{:S(2)}) collective-permute-start(bf16[2,2,32,512]{3,2,1,0:T(8,128)(2,1)S(1)} %collective-permute-done.1), channel_id=1, source_target_pairs={{0,1},{1,2},{2,3},{3,4},{4,5},{5,6},{6,7},{7,8},{8,9},{9,10},{10,1... | collective-permute-start | bytes 393224 | tf_op jit(solution)/shard_map/ppermute | solution.py:16
  30.7 7.1 %collective-permute-start.3 = (bf16[2,2,32,512]{3,2,1,0:T(8,128)(2,1)S(1)}, bf16[2,2,32,512]{3,2,1,0:T(8,128)(2,1)S(1)}, u32[]{:S(2)}, u32[]{:S(2)}) collective-permute-start(bf16[2,2,32,512]{3,2,1,0:T(8,128)(2,1)S(1)} %collective-permute-done.2), channel_id=1, source_target_pairs={{0,1},{1,2},{2,3},{3,4},{4,5},{5,6},{6,7},{7,8},{8,9},{9,10},{10,1... | collective-permute-start | bytes 393224 | tf_op jit(solution)/shard_map/ppermute | solution.py:16
  37.8 7.1 %collective-permute-start.4 = (bf16[2,2,32,512]{3,2,1,0:T(8,128)(2,1)S(1)}, bf16[2,2,32,512]{3,2,1,0:T(8,128)(2,1)S(1)}, u32[]{:S(2)}, u32[]{:S(2)}) collective-permute-start(bf16[2,2,32,512]{3,2,1,0:T(8,128)(2,1)S(1)} %collective-permute-done.3), channel_id=1, source_target_pairs={{0,1},{1,2},{2,3},{3,4},{4,5},{5,6},{6,7},{7,8},{8,9},{9,10},{10,1... | collective-permute-start | bytes 393224 | tf_op jit(solution)/shard_map/ppermute | solution.py:16
  44.9 7.1 %collective-permute-start.5 = (bf16[2,2,32,512]{3,2,1,0:T(8,128)(2,1)S(1)}, bf16[2,2,32,512]{3,2,1,0:T(8,128)(2,1)S(1)}, u32[]{:S(2)}, u32[]{:S(2)}) collective-permute-start(bf16[2,2,32,512]{3,2,1,0:T(8,128)(2,1)S(1)} %collective-permute-done.4), channel_id=1, source_target_pairs={{0,1},{1,2},{2,3},{3,4},{4,5},{5,6},{6,7},{7,8},{8,9},{9,10},{10,1... | collective-permute-start | bytes 393224 | tf_op jit(solution)/shard_map/ppermute | solution.py:16
  52.0 7.1 %collective-permute-start.6 = (bf16[2,2,32,512]{3,2,1,0:T(8,128)(2,1)S(1)}, bf16[2,2,32,512]{3,2,1,0:T(8,128)(2,1)S(1)}, u32[]{:S(2)}, u32[]{:S(2)}) collective-permute-start(bf16[2,2,32,512]{3,2,1,0:T(8,128)(2,1)S(1)} %collective-permute-done.5), channel_id=1, source_target_pairs={{0,1},{1,2},{2,3},{3,4},{4,5},{5,6},{6,7},{7,8},{8,9},{9,10},{10,1... | collective-permute-start | bytes 393224 | tf_op jit(solution)/shard_map/ppermute | solution.py:16
  59.1 7.1 %collective-permute-start.7 = (bf16[2,2,32,512]{3,2,1,0:T(8,128)(2,1)S(1)}, bf16[2,2,32,512]{3,2,1,0:T(8,128)(2,1)S(1)}, u32[]{:S(2)}, u32[]{:S(2)}) collective-permute-start(bf16[2,2,32,512]{3,2,1,0:T(8,128)(2,1)S(1)} %collective-permute-done.6), channel_id=1, source_target_pairs={{0,1},{1,2},{2,3},{3,4},{4,5},{5,6},{6,7},{7,8},{8,9},{9,10},{10,1... | collective-permute-start | bytes 393224 | tf_op jit(solution)/shard_map/ppermute | solution.py:16
  66.2 7.1 %collective-permute-start.8 = (bf16[2,2,32,512]{3,2,1,0:T(8,128)(2,1)S(1)}, bf16[2,2,32,512]{3,2,1,0:T(8,128)(2,1)S(1)}, u32[]{:S(2)}, u32[]{:S(2)}) collective-permute-start(bf16[2,2,32,512]{3,2,1,0:T(8,128)(2,1)S(1)} %collective-permute-done.7), channel_id=1, source_target_pairs={{0,1},{1,2},{2,3},{3,4},{4,5},{5,6},{6,7},{7,8},{8,9},{9,10},{10,1... | collective-permute-start | bytes 393224 | tf_op jit(solution)/shard_map/ppermute | solution.py:16
  73.3 7.1 %collective-permute-start.9 = (bf16[2,2,32,512]{3,2,1,0:T(8,128)(2,1)S(1)}, bf16[2,2,32,512]{3,2,1,0:T(8,128)(2,1)S(1)}, u32[]{:S(2)}, u32[]{:S(2)}) collective-permute-start(bf16[2,2,32,512]{3,2,1,0:T(8,128)(2,1)S(1)} %collective-permute-done.8), channel_id=1, source_target_pairs={{0,1},{1,2},{2,3},{3,4},{4,5},{5,6},{6,7},{7,8},{8,9},{9,10},{10,1... | collective-permute-start | bytes 393224 | tf_op jit(solution)/shard_map/ppermute | solution.py:16
  80.3 7.1 %collective-permute-start.10 = (bf16[2,2,32,512]{3,2,1,0:T(8,128)(2,1)S(1)}, bf16[2,2,32,512]{3,2,1,0:T(8,128)(2,1)S(1)}, u32[]{:S(2)}, u32[]{:S(2)}) collective-permute-start(bf16[2,2,32,512]{3,2,1,0:T(8,128)(2,1)S(1)} %collective-permute-done.9), channel_id=1, source_target_pairs={{0,1},{1,2},{2,3},{3,4},{4,5},{5,6},{6,7},{7,8},{8,9},{9,10},{10,1... | collective-permute-start | bytes 393224 | tf_op jit(solution)/shard_map/ppermute | solution.py:16
  87.4 7.1 %collective-permute-start.11 = (bf16[2,2,32,512]{3,2,1,0:T(8,128)(2,1)S(1)}, bf16[2,2,32,512]{3,2,1,0:T(8,128)(2,1)S(1)}, u32[]{:S(2)}, u32[]{:S(2)}) collective-permute-start(bf16[2,2,32,512]{3,2,1,0:T(8,128)(2,1)S(1)} %collective-permute-done.10), channel_id=1, source_target_pairs={{0,1},{1,2},{2,3},{3,4},{4,5},{5,6},{6,7},{7,8},{8,9},{9,10},{10,1... | collective-permute-start | bytes 393224 | tf_op jit(solution)/shard_map/ppermute | solution.py:16
  94.5 7.1 %collective-permute-start.12 = (bf16[2,2,32,512]{3,2,1,0:T(8,128)(2,1)S(1)}, bf16[2,2,32,512]{3,2,1,0:T(8,128)(2,1)S(1)}, u32[]{:S(2)}, u32[]{:S(2)}) collective-permute-start(bf16[2,2,32,512]{3,2,1,0:T(8,128)(2,1)S(1)} %collective-permute-done.11), channel_id=1, source_target_pairs={{0,1},{1,2},{2,3},{3,4},{4,5},{5,6},{6,7},{7,8},{8,9},{9,10},{10,1... | collective-permute-start | bytes 393224 | tf_op jit(solution)/shard_map/ppermute | solution.py:16
  101.6 7.1 %collective-permute-start.13 = (bf16[2,2,32,512]{3,2,1,0:T(8,128)(2,1)S(1)}, bf16[2,2,32,512]{3,2,1,0:T(8,128)(2,1)S(1)}, u32[]{:S(2)}, u32[]{:S(2)}) collective-permute-start(bf16[2,2,32,512]{3,2,1,0:T(8,128)(2,1)S(1)} %collective-permute-done.12), channel_id=1, source_target_pairs={{0,1},{1,2},{2,3},{3,4},{4,5},{5,6},{6,7},{7,8},{8,9},{9,10},{10,1... | collective-permute-start | bytes 393224 | tf_op jit(solution)/shard_map/ppermute | solution.py:16
  108.7 7.1 %collective-permute-start.14 = (bf16[2,2,32,512]{3,2,1,0:T(8,128)(2,1)S(1)}, bf16[2,2,32,512]{3,2,1,0:T(8,128)(2,1)S(1)}, u32[]{:S(2)}, u32[]{:S(2)}) collective-permute-start(bf16[2,2,32,512]{3,2,1,0:T(8,128)(2,1)S(1)} %collective-permute-done.13), channel_id=1, source_target_pairs={{0,1},{1,2},{2,3},{3,4},{4,5},{5,6},{6,7},{7,8},{8,9},{9,10},{10,1... | collective-permute-start | bytes 393224 | tf_op jit(solution)/shard_map/ppermute | solution.py:16
  116.7 10.5 %collective-permute-start.15 = (bf16[2,2,512,16]{3,2,1,0:T(8,128)(2,1)S(1)}, bf16[2,2,512,16]{3,2,1,0:T(8,128)(2,1)S(1)}, u32[]{:S(2)}, u32[]{:S(2)}) collective-permute-start(bf16[2,2,512,16]{3,2,1,0:T(8,128)(2,1)S(1)} %get-tuple-element.122), channel_id=1, source_target_pairs={{0,16},{1,17},{2,18},{3,19},{4,20},{5,21},{6,22},{7,23},{8,24},{9,... | collective-permute-start | bytes 196616 | tf_op jit(solution)/shard_map/ppermute | solution.py:27
  120.6 11.1 %collective-permute-start.16 = (bf16[2,2,512,16]{3,2,1,0:T(8,128)(2,1)S(1)}, bf16[2,2,512,16]{3,2,1,0:T(8,128)(2,1)S(1)}, u32[]{:S(2)}, u32[]{:S(2)}) collective-permute-start(bf16[2,2,512,16]{3,2,1,0:T(8,128)(2,1)S(1)} %get-tuple-element.123), channel_id=1, source_target_pairs={{16,0},{17,1},{18,2},{19,3},{20,4},{21,5},{22,6},{23,7},{24,8},{25... | collective-permute-start | bytes 196616 | tf_op jit(solution)/shard_map/ppermute | solution.py:30
Sparse Core Ops, SparseCore 0:
  425.9 89.9 all-reduce.2
